TPU v7x, 32 devices: a whole 2x2x4 slice. The times are simulated.
32 devices in a mesh: atom: 16 (over z, x, core), energy: 2 (over y).
Axes of the slice: x: 2, y: 2, z: 4, core: 2. Of those that a mesh axis runs over, the one named last changes fastest.
Arguments:
- single_site: float32 [256, 2, 2, 1024], P('atom', 'energy'), may hold values from -2 to 2
- structure: float32 [2, 26, 2, 1024], P('energy'), may hold values from -0.4375 to 0.4375
- neighbours: int32 [256, 26], P('atom'), may hold values from 0 to 255, as said below
- species: int32 [256], P('atom'), may hold values from 0 to 1
- valence: float32 [2], replicated, may hold values from 0.5 to 3
- energy_weights: float32 [2, 2], P('energy'), may hold values from -4 to 4
- gaunt_table: float32 [49, 1024], replicated, may hold values from -1.5 to 1.5
- radial_shapes: float32 [2, 2, 2, 49, 512], P(None, 'energy'), may hold values from -6 to 6
- radial_weights: float32 [512], replicated, may hold values from 0.001 to 0.03
- madelung: float32 [256, 256], P('atom'), may hold values from -0.375 to 0.375
- old_potential: float32 [256, 49, 512], P('atom', None, 'energy'), may hold values from -6 to 6
Outputs:
- density: float32 [256, 49, 512], P('atom', None, 'energy')
- potential: float32 [256, 49, 512], P('atom', None, 'energy')
Inputs may be any that keep to these rules, and one draw needn't show every extreme that they name: `neighbours`: atom a lies in lattice plane a // 16; the 16 planes close periodically. Slots 0 to 8 name distinct atoms of the plane before a's, slots 9 to 16 distinct atoms of a's own plane other than a, slots 17 to 25 distinct atoms of the plane after. Direction 26 - 1 - k is the reverse of direction k; this only says which structure constants pair up, and the neighbour lists need not be reciprocal.
All inputs are finite; a program needn't handle non-finite values.
Results may differ from a plain program's by a relative error of at most 0.0001.
Values sent between devices are 32-bit elements; how exact they have to be, the bound alone decides.
A program may use at most 64 MiB of HBM per device.

v0:
```python
import jax
import jax.numpy as jnp
from jax import lax
from jax.sharding import PartitionSpec as P

ORDER = 32
DIRS = 26
PLANE = 16
TERMS = 4
SPECIES = 2
mixing = 0.3
highest = lax.Precision.HIGHEST


def with_halo(block, sides, width):
    for axis, dim in sides:
        count = lax.axis_size(axis)
        forward = [(i, i + 1) for i in range(count - 1)]
        forward.append((count - 1, 0))
        backward = [(target, source) for source, target in forward]
        low = lax.ppermute(
            lax.slice_in_dim(block, block.shape[dim] - width, None, axis=dim), axis, forward
        )
        high = lax.ppermute(lax.slice_in_dim(block, 0, width, axis=dim), axis, backward)
        block = jnp.concatenate([low, block, high], axis=dim)
    return block


def matmul_high(former, latter):
    return jnp.matmul(former, latter, precision=highest)


def complex_product(former, latter):
    former_real = former[..., 0, :, :]
    former_imag = former[..., 1, :, :]
    latter_real = latter[..., 0, :, :]
    latter_imag = latter[..., 1, :, :]
    real_part = matmul_high(former_real, latter_real) - matmul_high(former_imag, latter_imag)
    imag_part = matmul_high(former_real, latter_imag) + matmul_high(former_imag, latter_real)
    return jnp.stack([real_part, imag_part], axis=-3)


def shards(
    single_site,
    structure,
    neighbours,
    species,
    valence,
    energy_weights,
    gaunt_table,
    radial_shapes,
    radial_weights,
    madelung,
    old_potential,
):
    atom_rows = single_site.shape[0]
    energy_rows = single_site.shape[1]
    extended = with_halo(single_site, (("atom", 0),), PLANE)
    extended = extended.reshape(extended.shape[0], energy_rows, 2, ORDER, ORDER)
    site_matrices = single_site.reshape(atom_rows, energy_rows, 2, ORDER, ORDER)
    couplings = structure.reshape(energy_rows, DIRS, 2, ORDER, ORDER)
    first_atom = lax.axis_index("atom") * atom_rows
    total_atoms = lax.axis_size("atom") * atom_rows
    local_rows = (neighbours - first_atom + PLANE) % total_atoms
    group_size = DIRS // 2
    forward_all = jnp.moveaxis(couplings, 1, 0)
    backward_all = forward_all[::-1]
    forward_groups = forward_all.reshape(2, group_size, energy_rows, 2, ORDER, ORDER)
    backward_groups = backward_all.reshape(2, group_size, energy_rows, 2, ORDER, ORDER)
    row_groups = jnp.transpose(local_rows).reshape(2, group_size, atom_rows)

    def add_group(accumulated, inputs):
        forward, backward, rows = inputs
        gathered = jnp.take(extended, rows, axis=0)
        left = complex_product(forward[:, None], gathered)
        terms = complex_product(left, backward[:, None])
        return (accumulated + jnp.sum(terms, axis=0), None)

    coupled, _ = lax.scan(
        add_group, jnp.zeros_like(site_matrices), (forward_groups, backward_groups, row_groups)
    )
    propagator = complex_product(site_matrices, coupled)
    series_term = site_matrices
    path_operator = site_matrices
    for power in range(TERMS - 1):
        series_term = complex_product(propagator, series_term)
        path_operator = path_operator + series_term
    flat = path_operator.reshape(atom_rows, energy_rows, 2, ORDER * ORDER)
    projected = jnp.einsum("aezq,lq->aezl", flat, gaunt_table, precision=highest)
    weight_real = energy_weights[:, 0][None, :, None]
    weight_imag = energy_weights[:, 1][None, :, None]
    scaled_real = weight_real * projected[:, :, 0] - weight_imag * projected[:, :, 1]
    scaled_imag = weight_real * projected[:, :, 1] + weight_imag * projected[:, :, 0]
    slice_width = old_potential.shape[2]
    energy_index = lax.axis_index("energy")
    kinds = jnp.arange(SPECIES, dtype=jnp.int32)
    one_hot = jnp.where(species[:, None] == kinds[None, :], jnp.float32(1.0), jnp.float32(0.0))
    valence_of = jnp.sum(one_hot * valence[None, :], axis=1)
    pieces = lax.all_to_all(radial_shapes, "energy", split_axis=4, concat_axis=1, tiled=True)
    all_real, all_imag = (
        lax.all_gather(scaled_real, "energy", axis=1, tiled=True),
        lax.all_gather(scaled_imag, "energy", axis=1, tiled=True),
    )
    sorted_real = one_hot[:, :, None, None] * all_real[:, None]
    sorted_imag = one_hot[:, :, None, None] * all_imag[:, None]
    density = jnp.einsum("asel,selr->alr", sorted_real, pieces[:, :, 1], precision=highest)
    density = density + jnp.einsum(
        "asel,selr->alr", sorted_imag, pieces[:, :, 0], precision=highest
    )
    piece_weights = lax.dynamic_slice_in_dim(
        radial_weights, energy_index * slice_width, slice_width
    )
    partial_charge = jnp.dot(density[:, 0, :], piece_weights, precision=highest)
    local_charge = lax.psum(partial_charge, "energy") - valence_of
    charges = lax.all_gather(local_charge, "atom", axis=0, tiled=True)
    madelung_shift = jnp.dot(madelung, charges, precision=highest)
    channel = jnp.arange(density.shape[1], dtype=jnp.int32)[None, :, None]
    added = jnp.where(channel == 0, madelung_shift[:, None, None], jnp.float32(0.0))
    potential = (1.0 - mixing) * old_potential + mixing * (density + added)
    return (density, potential)


def solution(mesh):
    in_specs = (
        P("atom", "energy", None, None),
        P("energy", None, None, None),
        P("atom", None),
        P("atom"),
        P(),
        P("energy", None),
        P(),
        P(None, "energy", None, None, None),
        P(),
        P("atom", None),
        P("atom", None, "energy"),
    )
    out_specs = (P("atom", None, "energy"), P("atom", None, "energy"))
    return jax.shard_map(shards, mesh=mesh, in_specs=in_specs, out_specs=out_specs, check_vma=False)
```

profile of v0, /device:TPU:0, one launch (start us, length us, event | category | flops | bytes accessed | tf_op | source)
XLA Modules:
  0.0 190.3 jit_solution(6027028950451602410)
XLA Ops:
  1.2 5.0 %collective-permute-start.1 = (f32[16,1,2,1024]{3,2,1,0:T(2,128)}, f32[16,1,2,1024]{3,2,1,0:T(2,128)S(1)}, u32[]{:S(2)}, u32[]{:S(2)}) collective-permute-start(f32[16,1,2,1024]{3,2,1,0:T(2,128)} %param.13), channel_id=1, source_target_pairs={{2,0},{4,2},{6,4},{8,6},{10,8},{12,10},{14,12},{16,14},{18,16},{20... | collective-permute-start | bytes 393224 | tf_op jit(solution)/shard_map/ppermute | solution.py:24
  6.3 1.6 copy.132
  7.9 2.5 %reshape.313 = f32[2,1,50176]{2,1,0:T(1,128)} reshape(f32[512,2,1,2,49]{4,3,2,1,0:T(2,128)S(1)} %bitcast.241) | data formatting | bytes 802816
  10.4 4.2 %all-to-all-start = ((f32[2,1,50176]{2,1,0:T(1,128)}), f32[2,1,50176]{2,1,0:T(1,128)}, u32[]{:S(2)}, u32[]{:S(2)}) async-start(f32[2,1,50176]{2,1,0:T(1,128)} %reshape.313), calls=%async_computation | async-start | bytes 802816 | tf_op jit(solution)/shard_map/all_to_all | solution.py:99
  23.6 100.0 %while.11 = (s32[]{:T(128)}, f32[16,1,2,32,32]{4,3,0,2,1:T(8,128)S(1)}, f32[2,13,1,2,32,32]{5,4,3,1,0,2:T(8,128)}, s32[2,13,16]{1,0,2:T(2,128)S(1)}, f32[48,1,2,...) while((s32[]{:T(128)}, ...), condition=%wide.region_2.3_spmd.clone, body=%wide.region_0.2_spmd.clone.sunk | while | flops 656476992 | bytes 64435708 | solution.py:79
  42.8 3.9 %gather_fusion = f32[208,2,32,32]{3,2,1,0:T(8,128)} fusion(f32[48,2,32,32]{3,2,1,0:T(8,128)S(1)} %bitcast.229, s32[1024]{0:T(1024)S(1)} %pad_clamp_fusion.2), kind=kCustom, calls=%fused_computation.clone.clone.1 | custom fusion | bytes 3408704 | tf_op jit(solution)/shard_map/while/body/eval_jaxpr/jit(_take)/gather | solution.py:74
  46.6 3.7 %copy.172 = f32[208,2,32,32]{3,2,0,1:T(8,128)S(1)} copy(f32[208,2,32,32]{3,2,1,0:T(8,128)} %gather_fusion) | data formatting | bytes 3407872 | tf_op jit(solution)/shard_map/while/body/eval_jaxpr/jit(_take)/gather | solution.py:74
  51.9 3.2 %fusion.81 = f32[13,32,16,32]{3,1,2,0:T(8,128)S(1)} fusion(f32[13,16,1,2,32,32]{5,4,1,0,3,2:T(8,128)S(1)} %broadcast_select_fusion.3, f32[13,1,1,2,32,32]{5,4,0,3,2,1:T(8,128)S(1)} %bitcast.235), kind=kOutput, calls=%fused_computation.16.clone.1 | convolution fusion | flops 81788928 | bytes 4472832 | tf_op jit(solution)/shard_map/while/body/eval_jaxpr/dot_general | solution.py:30
  55.1 3.3 %fusion.82 = f32[13,32,16,32]{3,1,2,0:T(8,128)S(1)} fusion(f32[13,32,16,32]{3,1,2,0:T(8,128)S(1)} %fusion.81, f32[13,16,1,2,32,32]{5,4,1,0,3,2:T(8,128)S(1)} %broadcast_select_fusion.3, f32[13,1,1,2,32,32]{5,4,0,3,2,1:T(8,128)S(1)} %bitcast.236), kind=kOutput, calls=%fused_computation.19.clone.1 | convolution fusion | flops 82001920 | bytes 7880704 | tf_op jit(solution)/shard_map/while/body/eval_jaxpr/dot_general | solution.py:30
  58.4 3.2 %fusion.78 = f32[13,32,16,32]{3,1,2,0:T(8,128)S(1)} fusion(f32[13,16,1,2,32,32]{5,4,1,0,3,2:T(8,128)S(1)} %broadcast_select_fusion.3, f32[13,1,1,2,32,32]{5,4,0,3,2,1:T(8,128)S(1)} %bitcast.237), kind=kOutput, calls=%fused_computation.15.clone.1 | convolution fusion | flops 81788928 | bytes 4472832 | tf_op jit(solution)/shard_map/while/body/eval_jaxpr/dot_general | solution.py:30
  61.6 3.3 %fusion.79 = f32[13,32,16,32]{3,1,2,0:T(8,128)S(1)} fusion(f32[13,32,16,32]{3,1,2,0:T(8,128)S(1)} %fusion.78, f32[13,16,1,2,32,32]{5,4,1,0,3,2:T(8,128)S(1)} %broadcast_select_fusion.3, f32[13,1,1,2,32,32]{5,4,0,3,2,1:T(8,128)S(1)} %bitcast.238), kind=kOutput, calls=%fused_computation.20.clone.1 | convolution fusion | flops 82001920 | bytes 7880704 | tf_op jit(solution)/shard_map/while/body/eval_jaxpr/dot_general | solution.py:30
  64.9 3.3 %fusion.83 = f32[13,16,32,32]{3,2,1,0:T(8,128)S(1)} fusion(f32[13,32,16,32]{3,1,2,0:T(8,128)S(1)} %fusion.79, f32[13,1,1,2,32,32]{5,4,0,3,2,1:T(8,128)S(1)} %bitcast.231), kind=kOutput, calls=%fused_computation.6.clone.1 | convolution fusion | flops 81788928 | bytes 4472832 | tf_op jit(solution)/shard_map/while/body/eval_jaxpr/dot_general | solution.py:30
  68.2 3.4 %subtract_bitcast_fusion.2 = f32[13,16,1,1,32,32]{5,4,1,0,3,2:T(8,128)S(1)} fusion(f32[13,16,32,32]{3,2,1,0:T(8,128)S(1)} %fusion.83, f32[13,32,16,32]{3,1,2,0:T(8,128)S(1)} %fusion.82, f32[13,1,1,2,32,32]{5,4,0,3,2,1:T(8,128)S(1)} %bitcast.232), kind=kOutput, calls=%fused_computation.13.clone.1 | convolution fusion | flops 82001920 | bytes 7880704 | tf_op jit(solution)/shard_map/while/body/eval_jaxpr/dot_general | solution.py:30
  71.6 3.3 %fusion.80 = f32[13,16,32,32]{3,2,1,0:T(8,128)S(1)} fusion(f32[13,32,16,32]{3,1,2,0:T(8,128)S(1)} %fusion.79, f32[13,1,1,2,32,32]{5,4,0,3,2,1:T(8,128)S(1)} %bitcast.233), kind=kOutput, calls=%fused_computation.4.clone.1 | convolution fusion | flops 81788928 | bytes 4472832 | tf_op jit(solution)/shard_map/while/body/eval_jaxpr/dot_general | solution.py:30
  74.9 3.4 %add_bitcast_fusion.2 = f32[13,16,1,1,32,32]{5,4,1,0,3,2:T(8,128)S(1)} fusion(f32[13,16,32,32]{3,2,1,0:T(8,128)S(1)} %fusion.80, f32[13,32,16,32]{3,1,2,0:T(8,128)S(1)} %fusion.82, f32[13,1,1,2,32,32]{5,4,0,3,2,1:T(8,128)S(1)} %bitcast.234), kind=kOutput, calls=%fused_computation.12.clone.1 | convolution fusion | flops 82001920 | bytes 7880704 | tf_op jit(solution)/shard_map/while/body/eval_jaxpr/dot_general | solution.py:30
  79.5 3.9 %gather_fusion = f32[208,2,32,32]{3,2,1,0:T(8,128)} fusion(f32[48,2,32,32]{3,2,1,0:T(8,128)S(1)} %bitcast.229, s32[1024]{0:T(1024)S(1)} %pad_clamp_fusion.2), kind=kCustom, calls=%fused_computation.clone.clone.1 | custom fusion | bytes 3408704 | tf_op jit(solution)/shard_map/while/body/eval_jaxpr/jit(_take)/gather | solution.py:74
  83.4 3.7 %copy.172 = f32[208,2,32,32]{3,2,0,1:T(8,128)S(1)} copy(f32[208,2,32,32]{3,2,1,0:T(8,128)} %gather_fusion) | data formatting | bytes 3407872 | tf_op jit(solution)/shard_map/while/body/eval_jaxpr/jit(_take)/gather | solution.py:74
  88.7 3.2 %fusion.81 = f32[13,32,16,32]{3,1,2,0:T(8,128)S(1)} fusion(f32[13,16,1,2,32,32]{5,4,1,0,3,2:T(8,128)S(1)} %broadcast_select_fusion.3, f32[13,1,1,2,32,32]{5,4,0,3,2,1:T(8,128)S(1)} %bitcast.235), kind=kOutput, calls=%fused_computation.16.clone.1 | convolution fusion | flops 81788928 | bytes 4472832 | tf_op jit(solution)/shard_map/while/body/eval_jaxpr/dot_general | solution.py:30
  91.9 3.3 %fusion.82 = f32[13,32,16,32]{3,1,2,0:T(8,128)S(1)} fusion(f32[13,32,16,32]{3,1,2,0:T(8,128)S(1)} %fusion.81, f32[13,16,1,2,32,32]{5,4,1,0,3,2:T(8,128)S(1)} %broadcast_select_fusion.3, f32[13,1,1,2,32,32]{5,4,0,3,2,1:T(8,128)S(1)} %bitcast.236), kind=kOutput, calls=%fused_computation.19.clone.1 | convolution fusion | flops 82001920 | bytes 7880704 | tf_op jit(solution)/shard_map/while/body/eval_jaxpr/dot_general | solution.py:30
  95.2 3.2 %fusion.78 = f32[13,32,16,32]{3,1,2,0:T(8,128)S(1)} fusion(f32[13,16,1,2,32,32]{5,4,1,0,3,2:T(8,128)S(1)} %broadcast_select_fusion.3, f32[13,1,1,2,32,32]{5,4,0,3,2,1:T(8,128)S(1)} %bitcast.237), kind=kOutput, calls=%fused_computation.15.clone.1 | convolution fusion | flops 81788928 | bytes 4472832 | tf_op jit(solution)/shard_map/while/body/eval_jaxpr/dot_general | solution.py:30
  98.4 3.3 %fusion.79 = f32[13,32,16,32]{3,1,2,0:T(8,128)S(1)} fusion(f32[13,32,16,32]{3,1,2,0:T(8,128)S(1)} %fusion.78, f32[13,16,1,2,32,32]{5,4,1,0,3,2:T(8,128)S(1)} %broadcast_select_fusion.3, f32[13,1,1,2,32,32]{5,4,0,3,2,1:T(8,128)S(1)} %bitcast.238), kind=kOutput, calls=%fused_computation.20.clone.1 | convolution fusion | flops 82001920 | bytes 7880704 | tf_op jit(solution)/shard_map/while/body/eval_jaxpr/dot_general | solution.py:30
  101.7 3.3 %fusion.83 = f32[13,16,32,32]{3,2,1,0:T(8,128)S(1)} fusion(f32[13,32,16,32]{3,1,2,0:T(8,128)S(1)} %fusion.79, f32[13,1,1,2,32,32]{5,4,0,3,2,1:T(8,128)S(1)} %bitcast.231), kind=kOutput, calls=%fused_computation.6.clone.1 | convolution fusion | flops 81788928 | bytes 4472832 | tf_op jit(solution)/shard_map/while/body/eval_jaxpr/dot_general | solution.py:30
  105.0 3.4 %subtract_bitcast_fusion.2 = f32[13,16,1,1,32,32]{5,4,1,0,3,2:T(8,128)S(1)} fusion(f32[13,16,32,32]{3,2,1,0:T(8,128)S(1)} %fusion.83, f32[13,32,16,32]{3,1,2,0:T(8,128)S(1)} %fusion.82, f32[13,1,1,2,32,32]{5,4,0,3,2,1:T(8,128)S(1)} %bitcast.232), kind=kOutput, calls=%fused_computation.13.clone.1 | convolution fusion | flops 82001920 | bytes 7880704 | tf_op jit(solution)/shard_map/while/body/eval_jaxpr/dot_general | solution.py:30
  108.3 3.3 %fusion.80 = f32[13,16,32,32]{3,2,1,0:T(8,128)S(1)} fusion(f32[13,32,16,32]{3,1,2,0:T(8,128)S(1)} %fusion.79, f32[13,1,1,2,32,32]{5,4,0,3,2,1:T(8,128)S(1)} %bitcast.233), kind=kOutput, calls=%fused_computation.4.clone.1 | convolution fusion | flops 81788928 | bytes 4472832 | tf_op jit(solution)/shard_map/while/body/eval_jaxpr/dot_general | solution.py:30
  111.6 3.4 %add_bitcast_fusion.2 = f32[13,16,1,1,32,32]{5,4,1,0,3,2:T(8,128)S(1)} fusion(f32[13,16,32,32]{3,2,1,0:T(8,128)S(1)} %fusion.80, f32[13,32,16,32]{3,1,2,0:T(8,128)S(1)} %fusion.82, f32[13,1,1,2,32,32]{5,4,0,3,2,1:T(8,128)S(1)} %bitcast.234), kind=kOutput, calls=%fused_computation.12.clone.1 | convolution fusion | flops 82001920 | bytes 7880704 | tf_op jit(solution)/shard_map/while/body/eval_jaxpr/dot_general | solution.py:30
  136.2 4.4 %all-gather.1 = f32[16,2,1,49]{3,0,2,1:T(8,128)S(1)} all-gather(f32[16,1,1,49]{3,0,2,1:T(8,128)S(1)} %get-tuple-element.89), channel_id=3, replica_groups=mesh['atom'=16,'energy'=2] {'energy'}, dimensions={1}, use_global_device_ids=true | all-gather | bytes 9408 | tf_op jit(solution)/shard_map/all_gather | solution.py:102
  140.6 4.6 %all-gather = f32[16,2,1,49]{3,0,2,1:T(8,128)S(1)} all-gather(f32[16,1,1,49]{3,0,2,1:T(8,128)S(1)} %get-tuple-element.88), channel_id=2, replica_groups=mesh['atom'=16,'energy'=2] {'energy'}, dimensions={1}, use_global_device_ids=true | all-gather | bytes 9408 | tf_op jit(solution)/shard_map/all_gather | solution.py:101
  145.8 2.8 %reduce.1 = f32[2,50176]{1,0:T(2,128)S(1)} reduce(f32[2,1,50176]{2,1,0:T(1,128)} %all-to-all-done, f32[]{:T(128)} %broadcast.157), dimensions={1}, to_apply=%all_to_all.13.reduce_sub_computation | reduce | bytes 802820 | tf_op jit(solution)/shard_map/all_to_all | solution.py:99
  148.6 1.8 reshape.314
  153.1 4.9 %psum.7 = f32[16]{0:T(128)S(1)} all-reduce(f32[16]{0:T(128)S(1)} %convolution_bitcast_fusion.4), channel_id=1, replica_groups=mesh['atom'=16,'energy'=2] {'energy'}, use_global_device_ids=true, to_apply=%region_3.4 | all-reduce | flops 16 | bytes 128 | tf_op jit(solution)/shard_map/psum | solution.py:114
  158.1 29.5 %all-reduce = f32[256]{0:T(256)S(1)} all-reduce(f32[256]{0:T(256)S(1)} %subtract_dynamic-update-slice_fusion), channel_id=1, replica_groups=mesh['atom'=16,'energy'=2] {'atom'}, use_global_device_ids=true, to_apply=%add | all-reduce | flops 256 | bytes 2048
  187.8 2.2 %multiply_add_fusion = f32[16,49,256]{2,0,1:T(8,128)} fusion(f32[16,49,256]{2,0,1:T(8,128)S(1)} %fusion.19, f32[16,49,256]{2,0,1:T(8,128)} %param.23, f32[16,49]{0,1:T(8,128)S(1)} %broadcast_select_fusion.1), kind=kLoop, calls=%fused_computation.50 | loop fusion | flops 802816 | bytes 2411584 | tf_op jit(solution)/shard_map/add | solution.py:119
  (122 shorter events, 30.3 us)
Async XLA Ops:
  0.6 134.0 %copy-start = (f32[49,1024]{1,0:T(8,128)S(1)}, f32[49,1024]{1,0:T(8,128)}, u32[]{:S(2)}) copy-start(f32[49,1024]{1,0:T(8,128)} %param.19) | copy-start | bytes 602116
  0.6 15.7 %copy-start.5 = (f32[16,1,2,1024]{3,2,1,0:T(2,128)S(1)}, f32[16,1,2,1024]{3,2,1,0:T(2,128)}, u32[]{:S(2)}) copy-start(f32[16,1,2,1024]{3,2,1,0:T(2,128)} %param.13) | copy-start | bytes 393220
  0.7 13.9 %copy-start.10 = (s32[16,26]{1,0:T(8,128)S(1)}, s32[16,26]{1,0:T(8,128)}, u32[]{:S(2)}) copy-start(s32[16,26]{1,0:T(8,128)} %param.15) | copy-start | bytes 4996
  0.7 14.0 %copy-start.15 = (s32[16]{0:T(128)S(1)}, s32[16]{0:T(128)}, u32[]{:S(2)}) copy-start(s32[16]{0:T(128)} %param.16) | copy-start | bytes 196
  0.7 14.0 %copy-start.14 = (f32[2]{0:T(128)S(1)}, f32[2]{0:T(128)}, u32[]{:S(2)}) copy-start(f32[2]{0:T(128)} %param.17) | copy-start | bytes 28
  0.7 15.7 %copy-start.7 = (f32[1,26,2,1024]{3,2,1,0:T(2,128)S(1)}, f32[1,26,2,1024]{3,2,1,0:T(2,128)}, u32[]{:S(2)}) copy-start(f32[1,26,2,1024]{3,2,1,0:T(2,128)} %param.14) | copy-start | bytes 638980
  0.7 22.0 %collective-permute-start = (f32[16,1,2,1024]{3,2,1,0:T(2,128)}, f32[16,1,2,1024]{3,2,1,0:T(2,128)S(1)}, u32[]{:S(2)}, u32[]{:S(2)}) collective-permute-start(f32[16,1,2,1024]{3,2,1,0:T(2,128)} %param.13), channel_id=1, source_target_pairs={{0,2},{2,4},{4,6},{6,8},{8,10},{10,12},{12,14},{14,16},{16,18},{18... | collective-permute-start | bytes 393224 | tf_op jit(solution)/shard_map/ppermute | solution.py:21
  1.2 21.5 %collective-permute-start.1 = (f32[16,1,2,1024]{3,2,1,0:T(2,128)}, f32[16,1,2,1024]{3,2,1,0:T(2,128)S(1)}, u32[]{:S(2)}, u32[]{:S(2)}) collective-permute-start(f32[16,1,2,1024]{3,2,1,0:T(2,128)} %param.13), channel_id=1, source_target_pairs={{2,0},{4,2},{6,4},{8,6},{10,8},{12,10},{14,12},{16,14},{18,16},{20... | collective-permute-start | bytes 393224 | tf_op jit(solution)/shard_map/ppermute | solution.py:24
  7.9 12.3 %copy-start.16 = (f32[512]{0:T(512)S(1)}, f32[512]{0:T(512)}, u32[]{:S(2)}) copy-start(f32[512]{0:T(512)} %param.21) | copy-start | bytes 6148
  7.9 12.9 %copy-start.18 = (u32[32]{0:T(128)S(1)}, u32[32]{0:T(128)}, u32[]{:S(2)}) copy-start(u32[32]{0:T(128)} %constant.72) | copy-start | bytes 388
  7.9 14.2 %copy-start.12 = (f32[1,2]{1,0:T(1,128)S(1)}, f32[1,2]{1,0:T(1,128)}, u32[]{:S(2)}) copy-start(f32[1,2]{1,0:T(1,128)} %param.18) | copy-start | bytes 28
  10.4 134.9 %all-to-all-start = ((f32[2,1,50176]{2,1,0:T(1,128)}), f32[2,1,50176]{2,1,0:T(1,128)}, u32[]{:S(2)}, u32[]{:S(2)}) async-start(f32[2,1,50176]{2,1,0:T(1,128)} %reshape.313), calls=%async_computation | async-start | bytes 802816 | tf_op jit(solution)/shard_map/all_to_all | solution.py:99
  23.6 100.3 %copy-start.1 = (f32[16,1,2,32,32]{4,3,0,2,1:T(8,128)S(1)}, f32[16,1,2,32,32]{4,3,0,2,1:T(8,128)}, u32[]{:S(2)}) copy-start(f32[16,1,2,32,32]{4,3,0,2,1:T(8,128)} %reshape.276) | copy-start | bytes 393220
  50.4 1.2 copy-start.2
  50.4 1.4 copy-start.3
  87.1 1.2 copy-start.2
  87.1 1.4 copy-start.3
  130.3 4.0 %copy-start.6 = (f32[16,1,2,1024]{3,2,1,0:T(2,128)S(1)}, f32[16,1,2,1024]{3,2,1,0:T(2,128)}, u32[]{:S(2)}) copy-start(f32[16,1,2,1024]{3,2,1,0:T(2,128)} %param.13) | copy-start | bytes 393220
  133.4 17.7 %copy-start.9 = (f32[16,2]{0,1:T(2,128)S(1)}, f32[16,2]{0,1:T(2,128)}, u32[]{:S(2)}) copy-start(f32[16,2]{0,1:T(2,128)} %get-tuple-element.91) | copy-start | bytes 388
  136.1 16.8 %copy-start.11 = (f32[256]{0:T(256)S(1)}, f32[256]{0:T(256)}, u32[]{:S(2)}) copy-start(f32[256]{0:T(256)} %dynamic_slice.14) | copy-start | bytes 3076
  140.5 17.5 %copy-start.13 = (f32[16]{0:T(128)S(1)}, f32[16]{0:T(128)}, u32[]{:S(2)}) copy-start(f32[16]{0:T(128)} %get-tuple-element.90) | copy-start | bytes 196
  140.5 47.1 %copy-start.8 = (f32[16,256]{1,0:T(8,128)S(1)}, f32[16,256]{1,0:T(8,128)}, u32[]{:S(2)}) copy-start(f32[16,256]{1,0:T(8,128)} %param.22) | copy-start | bytes 49156
  140.5 47.2 %copy-start.17 = (pred[49]{0:T(512)(128)(4,1)S(1)}, pred[49]{0:T(512)(128)(4,1)}, u32[]{:S(2)}) copy-start(pred[49]{0:T(512)(128)(4,1)} %iota_compare_fusion) | copy-start | bytes 151
  153.0 37.1 %copy-start.4 = (f32[16,49,256]{2,0,1:T(8,128)}, f32[16,49,256]{2,0,1:T(8,128)S(1)}, u32[]{:S(2)}) copy-start(f32[16,49,256]{2,0,1:T(8,128)S(1)} %fusion.19) | copy-start | bytes 2408452
where the time goes:
time: 194 us; the launch traced here: 190 us
  matrix products  64.2 us (33%)
  blocking collectives  43.3 us (22%)
  local copies, waits for them, and re-layouts  32.3 us (17%)
  loops' own time  26.8 us (14%)
  other arithmetic  11.9 us (6%)
  starting transfers between devices  9.73 us (5%)
  between operations  2.05 us (1%)
    dot_general x32, matrix products, matmul_high(): return jnp.matmul(former, latter, precision=highest)  61.7 us
    unnamed x1, blocking collectives  29.5 us
    another operation x1, loops' own time, shards(): lax.scan(add_group, jnp.zeros_like(site_matrices), (forward_groups, backw...  26.8 us
    gather x4, local copies, waits for them, and re-layouts, add_group(): gathered = jnp.take(extended, rows, axis=0)  15.2 us
    unnamed x40, local copies, waits for them, and re-layouts  6.71 us
    ppermute x1, starting transfers between devices, with_halo(): lax.ppermute(lax.slice_in_dim(block, 0, width, axis=dim), axis, backward)  5.02 us
    psum x1, blocking collectives, shards(): local_charge = lax.psum(partial_charge, 'energy') - valence_of  4.92 us
    all_gather x1, blocking collectives, shards(): lax.all_gather(scaled_real, 'energy', axis=1, tiled=True)  4.56 us
  transfers between devices with their start and end apart: 3, of which 0 were waited for; matrix products, arithmetic and copies ran while one was open for 51% of the time, Pallas kernels for 0%

commit v1 on v0

--- a/solution.py
+++ b/solution.py
@@ -96,7 +96,12 @@
     kinds = jnp.arange(SPECIES, dtype=jnp.int32)
     one_hot = jnp.where(species[:, None] == kinds[None, :], jnp.float32(1.0), jnp.float32(0.0))
     valence_of = jnp.sum(one_hot * valence[None, :], axis=1)
-    pieces = lax.all_to_all(radial_shapes, "energy", split_axis=4, concat_axis=1, tiled=True)
+    pieces = jnp.concatenate(
+        lax.all_to_all(
+            jnp.stack(jnp.split(radial_shapes, lax.axis_size("energy"), axis=4)), "energy", 0, 0
+        ),
+        axis=1,
+    )
     all_real, all_imag = (
         lax.all_gather(scaled_real, "energy", axis=1, tiled=True),
         lax.all_gather(scaled_imag, "energy", axis=1, tiled=True),

time: 194 us -> 188 us (0.969)
  local copies, waits for them, and re-layouts: 32.3 us -> 28.6 us
    unnamed x40 -> x33, local copies, waits for them, and re-layouts: 6.71 us -> 1.64 us
    all_to_all x1 -> x0, other arithmetic: 2.81 us -> none  [shards(): lax.all_to_all(radial_shapes, 'energy', split_axis=4, concat_axis=1, tile...]
  transfers between devices with their start and end apart: 3 -> 3, of which waited for: 0 -> 0; matrix products, arithmetic and copies ran while one was open for 51% -> 52% of each run, Pallas kernels for 0% -> 0%
where the time goes in v1:
time: 188 us; the launch traced here: 185 us
  matrix products  64.1 us (34%)
  blocking collectives  43.3 us (23%)
  local copies, waits for them, and re-layouts  28.6 us (15%)
  loops' own time  26.8 us (14%)
  other arithmetic  10.3 us (5%)
  starting transfers between devices  9.73 us (5%)
  between operations  1.96 us (1%)
    dot_general x32, matrix products, matmul_high(): return jnp.matmul(former, latter, precision=highest)  61.7 us
    unnamed x1, blocking collectives  29.5 us
    another operation x1, loops' own time, shards(): lax.scan(add_group, jnp.zeros_like(site_matrices), (forward_groups, backw...  26.8 us
    gather x4, local copies, waits for them, and re-layouts, add_group(): gathered = jnp.take(extended, rows, axis=0)  15.2 us
    ppermute x1, starting transfers between devices, with_halo(): lax.ppermute(lax.slice_in_dim(block, 0, width, axis=dim), axis, backward)  5.02 us
    psum x1, blocking collectives, shards(): local_charge = lax.psum(partial_charge, 'energy') - valence_of  4.92 us
    all_gather x1, blocking collectives, shards(): lax.all_gather(scaled_real, 'energy', axis=1, tiled=True)  4.56 us
    all_gather x1, blocking collectives, shards(): lax.all_gather(scaled_imag, 'energy', axis=1, tiled=True)  4.36 us
  transfers between devices with their start and end apart: 3, of which 0 were waited for; matrix products, arithmetic and copies ran while one was open for 52% of the time, Pallas kernels for 0%

profile of v1, /device:TPU:0, one launch (start us, length us, event | category | flops | bytes accessed | tf_op | source)
XLA Modules:
  0.0 184.9 jit_solution(8031446700648571190)
XLA Ops:
  1.2 5.0 %collective-permute-start.1 = (f32[16,1,2,1024]{3,2,1,0:T(2,128)}, f32[16,1,2,1024]{3,2,1,0:T(2,128)S(1)}, u32[]{:S(2)}, u32[]{:S(2)}) collective-permute-start(f32[16,1,2,1024]{3,2,1,0:T(2,128)} %param.13), channel_id=1, source_target_pairs={{2,0},{4,2},{6,4},{8,6},{10,8},{12,10},{14,12},{16,14},{18,16},{20... | collective-permute-start | bytes 393224 | tf_op jit(solution)/shard_map/ppermute | solution.py:24
  6.2 1.2 fusion.36
  8.6 4.2 %all-to-all-start = ((f32[2,2,1,2,49,256]{5,1,4,3,2,0:T(2,128)}), f32[2,2,1,2,49,256]{5,1,4,3,2,0:T(2,128)}, u32[]{:S(2)}, u32[]{:S(2)}) async-start(f32[2,2,1,2,49,256]{5,1,4,3,2,0:T(2,128)} %pad_maximum_fusion), calls=%async_computation | async-start | bytes 802816 | tf_op jit(solution)/shard_map/all_to_all | solution.py:100
  13.5 1.8 multiply_reduce_fusion
  17.1 1.3 reshape_transpose_reshape.3
  23.8 100.1 %while.11 = (s32[]{:T(128)}, f32[16,1,2,32,32]{4,3,0,2,1:T(8,128)S(1)}, f32[2,13,1,2,32,32]{5,4,3,1,0,2:T(8,128)}, s32[2,13,16]{1,0,2:T(2,128)S(1)}, f32[48,1,2,...) while((s32[]{:T(128)}, ...), condition=%wide.region_2.3_spmd.clone, body=%wide.region_0.2_spmd.clone.sunk | while | flops 656476992 | bytes 64435708 | solution.py:79
  43.0 3.9 %gather_fusion = f32[208,2,32,32]{3,2,1,0:T(8,128)} fusion(f32[48,2,32,32]{3,2,1,0:T(8,128)S(1)} %bitcast.232, s32[1024]{0:T(1024)S(1)} %pad_clamp_fusion.2), kind=kCustom, calls=%fused_computation.clone.clone.1 | custom fusion | bytes 3408704 | tf_op jit(solution)/shard_map/while/body/eval_jaxpr/jit(_take)/gather | solution.py:74
  46.8 3.7 %copy.146 = f32[208,2,32,32]{3,2,0,1:T(8,128)S(1)} copy(f32[208,2,32,32]{3,2,1,0:T(8,128)} %gather_fusion) | data formatting | bytes 3407872 | tf_op jit(solution)/shard_map/while/body/eval_jaxpr/jit(_take)/gather | solution.py:74
  52.1 3.2 %fusion.82 = f32[13,32,16,32]{3,1,2,0:T(8,128)S(1)} fusion(f32[13,16,1,2,32,32]{5,4,1,0,3,2:T(8,128)S(1)} %broadcast_select_fusion.3, f32[13,1,1,2,32,32]{5,4,0,3,2,1:T(8,128)S(1)} %bitcast.238), kind=kOutput, calls=%fused_computation.16.clone.1 | convolution fusion | flops 81788928 | bytes 4472832 | tf_op jit(solution)/shard_map/while/body/eval_jaxpr/dot_general | solution.py:30
  55.3 3.3 %fusion.83 = f32[13,32,16,32]{3,1,2,0:T(8,128)S(1)} fusion(f32[13,32,16,32]{3,1,2,0:T(8,128)S(1)} %fusion.82, f32[13,16,1,2,32,32]{5,4,1,0,3,2:T(8,128)S(1)} %broadcast_select_fusion.3, f32[13,1,1,2,32,32]{5,4,0,3,2,1:T(8,128)S(1)} %bitcast.239), kind=kOutput, calls=%fused_computation.19.clone.1 | convolution fusion | flops 82001920 | bytes 7880704 | tf_op jit(solution)/shard_map/while/body/eval_jaxpr/dot_general | solution.py:30
  58.6 3.2 %fusion.79 = f32[13,32,16,32]{3,1,2,0:T(8,128)S(1)} fusion(f32[13,16,1,2,32,32]{5,4,1,0,3,2:T(8,128)S(1)} %broadcast_select_fusion.3, f32[13,1,1,2,32,32]{5,4,0,3,2,1:T(8,128)S(1)} %bitcast.240), kind=kOutput, calls=%fused_computation.15.clone.1 | convolution fusion | flops 81788928 | bytes 4472832 | tf_op jit(solution)/shard_map/while/body/eval_jaxpr/dot_general | solution.py:30
  61.8 3.3 %fusion.80 = f32[13,32,16,32]{3,1,2,0:T(8,128)S(1)} fusion(f32[13,32,16,32]{3,1,2,0:T(8,128)S(1)} %fusion.79, f32[13,16,1,2,32,32]{5,4,1,0,3,2:T(8,128)S(1)} %broadcast_select_fusion.3, f32[13,1,1,2,32,32]{5,4,0,3,2,1:T(8,128)S(1)} %bitcast.241), kind=kOutput, calls=%fused_computation.20.clone.1 | convolution fusion | flops 82001920 | bytes 7880704 | tf_op jit(solution)/shard_map/while/body/eval_jaxpr/dot_general | solution.py:30
  65.2 3.3 %fusion.84 = f32[13,16,32,32]{3,2,1,0:T(8,128)S(1)} fusion(f32[13,32,16,32]{3,1,2,0:T(8,128)S(1)} %fusion.80, f32[13,1,1,2,32,32]{5,4,0,3,2,1:T(8,128)S(1)} %bitcast.234), kind=kOutput, calls=%fused_computation.6.clone.1 | convolution fusion | flops 81788928 | bytes 4472832 | tf_op jit(solution)/shard_map/while/body/eval_jaxpr/dot_general | solution.py:30
  68.4 3.4 %subtract_bitcast_fusion.2 = f32[13,16,1,1,32,32]{5,4,1,0,3,2:T(8,128)S(1)} fusion(f32[13,16,32,32]{3,2,1,0:T(8,128)S(1)} %fusion.84, f32[13,32,16,32]{3,1,2,0:T(8,128)S(1)} %fusion.83, f32[13,1,1,2,32,32]{5,4,0,3,2,1:T(8,128)S(1)} %bitcast.235), kind=kOutput, calls=%fused_computation.13.clone.1 | convolution fusion | flops 82001920 | bytes 7880704 | tf_op jit(solution)/shard_map/while/body/eval_jaxpr/dot_general | solution.py:30
  71.8 3.3 %fusion.81 = f32[13,16,32,32]{3,2,1,0:T(8,128)S(1)} fusion(f32[13,32,16,32]{3,1,2,0:T(8,128)S(1)} %fusion.80, f32[13,1,1,2,32,32]{5,4,0,3,2,1:T(8,128)S(1)} %bitcast.236), kind=kOutput, calls=%fused_computation.4.clone.1 | convolution fusion | flops 81788928 | bytes 4472832 | tf_op jit(solution)/shard_map/while/body/eval_jaxpr/dot_general | solution.py:30
  75.1 3.4 %add_bitcast_fusion.2 = f32[13,16,1,1,32,32]{5,4,1,0,3,2:T(8,128)S(1)} fusion(f32[13,16,32,32]{3,2,1,0:T(8,128)S(1)} %fusion.81, f32[13,32,16,32]{3,1,2,0:T(8,128)S(1)} %fusion.83, f32[13,1,1,2,32,32]{5,4,0,3,2,1:T(8,128)S(1)} %bitcast.237), kind=kOutput, calls=%fused_computation.12.clone.1 | convolution fusion | flops 82001920 | bytes 7880704 | tf_op jit(solution)/shard_map/while/body/eval_jaxpr/dot_general | solution.py:30
  79.8 3.9 %gather_fusion = f32[208,2,32,32]{3,2,1,0:T(8,128)} fusion(f32[48,2,32,32]{3,2,1,0:T(8,128)S(1)} %bitcast.232, s32[1024]{0:T(1024)S(1)} %pad_clamp_fusion.2), kind=kCustom, calls=%fused_computation.clone.clone.1 | custom fusion | bytes 3408704 | tf_op jit(solution)/shard_map/while/body/eval_jaxpr/jit(_take)/gather | solution.py:74
  83.6 3.7 %copy.146 = f32[208,2,32,32]{3,2,0,1:T(8,128)S(1)} copy(f32[208,2,32,32]{3,2,1,0:T(8,128)} %gather_fusion) | data formatting | bytes 3407872 | tf_op jit(solution)/shard_map/while/body/eval_jaxpr/jit(_take)/gather | solution.py:74
  88.9 3.2 %fusion.82 = f32[13,32,16,32]{3,1,2,0:T(8,128)S(1)} fusion(f32[13,16,1,2,32,32]{5,4,1,0,3,2:T(8,128)S(1)} %broadcast_select_fusion.3, f32[13,1,1,2,32,32]{5,4,0,3,2,1:T(8,128)S(1)} %bitcast.238), kind=kOutput, calls=%fused_computation.16.clone.1 | convolution fusion | flops 81788928 | bytes 4472832 | tf_op jit(solution)/shard_map/while/body/eval_jaxpr/dot_general | solution.py:30
  92.1 3.3 %fusion.83 = f32[13,32,16,32]{3,1,2,0:T(8,128)S(1)} fusion(f32[13,32,16,32]{3,1,2,0:T(8,128)S(1)} %fusion.82, f32[13,16,1,2,32,32]{5,4,1,0,3,2:T(8,128)S(1)} %broadcast_select_fusion.3, f32[13,1,1,2,32,32]{5,4,0,3,2,1:T(8,128)S(1)} %bitcast.239), kind=kOutput, calls=%fused_computation.19.clone.1 | convolution fusion | flops 82001920 | bytes 7880704 | tf_op jit(solution)/shard_map/while/body/eval_jaxpr/dot_general | solution.py:30
  95.4 3.2 %fusion.79 = f32[13,32,16,32]{3,1,2,0:T(8,128)S(1)} fusion(f32[13,16,1,2,32,32]{5,4,1,0,3,2:T(8,128)S(1)} %broadcast_select_fusion.3, f32[13,1,1,2,32,32]{5,4,0,3,2,1:T(8,128)S(1)} %bitcast.240), kind=kOutput, calls=%fused_computation.15.clone.1 | convolution fusion | flops 81788928 | bytes 4472832 | tf_op jit(solution)/shard_map/while/body/eval_jaxpr/dot_general | solution.py:30
  98.6 3.3 %fusion.80 = f32[13,32,16,32]{3,1,2,0:T(8,128)S(1)} fusion(f32[13,32,16,32]{3,1,2,0:T(8,128)S(1)} %fusion.79, f32[13,16,1,2,32,32]{5,4,1,0,3,2:T(8,128)S(1)} %broadcast_select_fusion.3, f32[13,1,1,2,32,32]{5,4,0,3,2,1:T(8,128)S(1)} %bitcast.241), kind=kOutput, calls=%fused_computation.20.clone.1 | convolution fusion | flops 82001920 | bytes 7880704 | tf_op jit(solution)/shard_map/while/body/eval_jaxpr/dot_general | solution.py:30
  101.9 3.3 %fusion.84 = f32[13,16,32,32]{3,2,1,0:T(8,128)S(1)} fusion(f32[13,32,16,32]{3,1,2,0:T(8,128)S(1)} %fusion.80, f32[13,1,1,2,32,32]{5,4,0,3,2,1:T(8,128)S(1)} %bitcast.234), kind=kOutput, calls=%fused_computation.6.clone.1 | convolution fusion | flops 81788928 | bytes 4472832 | tf_op jit(solution)/shard_map/while/body/eval_jaxpr/dot_general | solution.py:30
  105.2 3.4 %subtract_bitcast_fusion.2 = f32[13,16,1,1,32,32]{5,4,1,0,3,2:T(8,128)S(1)} fusion(f32[13,16,32,32]{3,2,1,0:T(8,128)S(1)} %fusion.84, f32[13,32,16,32]{3,1,2,0:T(8,128)S(1)} %fusion.83, f32[13,1,1,2,32,32]{5,4,0,3,2,1:T(8,128)S(1)} %bitcast.235), kind=kOutput, calls=%fused_computation.13.clone.1 | convolution fusion | flops 82001920 | bytes 7880704 | tf_op jit(solution)/shard_map/while/body/eval_jaxpr/dot_general | solution.py:30
  108.6 3.3 %fusion.81 = f32[13,16,32,32]{3,2,1,0:T(8,128)S(1)} fusion(f32[13,32,16,32]{3,1,2,0:T(8,128)S(1)} %fusion.80, f32[13,1,1,2,32,32]{5,4,0,3,2,1:T(8,128)S(1)} %bitcast.236), kind=kOutput, calls=%fused_computation.4.clone.1 | convolution fusion | flops 81788928 | bytes 4472832 | tf_op jit(solution)/shard_map/while/body/eval_jaxpr/dot_general | solution.py:30
  111.9 3.4 %add_bitcast_fusion.2 = f32[13,16,1,1,32,32]{5,4,1,0,3,2:T(8,128)S(1)} fusion(f32[13,16,32,32]{3,2,1,0:T(8,128)S(1)} %fusion.81, f32[13,32,16,32]{3,1,2,0:T(8,128)S(1)} %fusion.83, f32[13,1,1,2,32,32]{5,4,0,3,2,1:T(8,128)S(1)} %bitcast.237), kind=kOutput, calls=%fused_computation.12.clone.1 | convolution fusion | flops 82001920 | bytes 7880704 | tf_op jit(solution)/shard_map/while/body/eval_jaxpr/dot_general | solution.py:30
  135.2 1.3 multiply_subtract_fusion
  136.6 4.4 %all-gather.1 = f32[16,2,1,49]{3,0,2,1:T(8,128)S(1)} all-gather(f32[16,1,1,49]{3,0,2,1:T(8,128)S(1)} %get-tuple-element.85), channel_id=3, replica_groups=mesh['atom'=16,'energy'=2] {'energy'}, dimensions={1}, use_global_device_ids=true | all-gather | bytes 9408 | tf_op jit(solution)/shard_map/all_gather | solution.py:107
  141.1 4.6 %all-gather = f32[16,2,1,49]{3,0,2,1:T(8,128)S(1)} all-gather(f32[16,1,1,49]{3,0,2,1:T(8,128)S(1)} %get-tuple-element.84), channel_id=2, replica_groups=mesh['atom'=16,'energy'=2] {'energy'}, dimensions={1}, use_global_device_ids=true | all-gather | bytes 9408 | tf_op jit(solution)/shard_map/all_gather | solution.py:106
  145.7 1.1 copy.140
  148.9 4.9 %psum.7 = f32[16]{0:T(128)S(1)} all-reduce(f32[16]{0:T(128)S(1)} %convolution_bitcast_fusion.4), channel_id=1, replica_groups=mesh['atom'=16,'energy'=2] {'energy'}, use_global_device_ids=true, to_apply=%region_3.4 | all-reduce | flops 16 | bytes 128 | tf_op jit(solution)/shard_map/psum | solution.py:119
  153.9 29.5 %all-reduce = f32[256]{0:T(256)S(1)} all-reduce(f32[256]{0:T(256)S(1)} %subtract_dynamic-update-slice_fusion), channel_id=1, replica_groups=mesh['atom'=16,'energy'=2] {'atom'}, use_global_device_ids=true, to_apply=%add | all-reduce | flops 256 | bytes 2048
  (116 shorter events, 29.3 us)
Async XLA Ops:
  0.6 134.3 %copy-start = (f32[49,1024]{1,0:T(8,128)S(1)}, f32[49,1024]{1,0:T(8,128)}, u32[]{:S(2)}) copy-start(f32[49,1024]{1,0:T(8,128)} %param.19) | copy-start | bytes 602116
  0.6 16.1 %copy-start.7 = (f32[1,26,2,1024]{3,2,1,0:T(2,128)S(1)}, f32[1,26,2,1024]{3,2,1,0:T(2,128)}, u32[]{:S(2)}) copy-start(f32[1,26,2,1024]{3,2,1,0:T(2,128)} %param.14) | copy-start | bytes 638980
  0.7 22.3 %collective-permute-start = (f32[16,1,2,1024]{3,2,1,0:T(2,128)}, f32[16,1,2,1024]{3,2,1,0:T(2,128)S(1)}, u32[]{:S(2)}, u32[]{:S(2)}) collective-permute-start(f32[16,1,2,1024]{3,2,1,0:T(2,128)} %param.13), channel_id=1, source_target_pairs={{0,2},{2,4},{4,6},{6,8},{8,10},{10,12},{12,14},{14,16},{16,18},{18... | collective-permute-start | bytes 393224 | tf_op jit(solution)/shard_map/ppermute | solution.py:21
  1.2 21.7 %collective-permute-start.1 = (f32[16,1,2,1024]{3,2,1,0:T(2,128)}, f32[16,1,2,1024]{3,2,1,0:T(2,128)S(1)}, u32[]{:S(2)}, u32[]{:S(2)}) collective-permute-start(f32[16,1,2,1024]{3,2,1,0:T(2,128)} %param.13), channel_id=1, source_target_pairs={{2,0},{4,2},{6,4},{8,6},{10,8},{12,10},{14,12},{16,14},{18,16},{20... | collective-permute-start | bytes 393224 | tf_op jit(solution)/shard_map/ppermute | solution.py:24
  7.6 12.9 %copy-start.14 = (f32[512]{0:T(512)S(1)}, f32[512]{0:T(512)}, u32[]{:S(2)}) copy-start(f32[512]{0:T(512)} %param.21) | copy-start | bytes 6148
  7.6 13.5 %copy-start.16 = (u32[32]{0:T(128)S(1)}, u32[32]{0:T(128)}, u32[]{:S(2)}) copy-start(u32[32]{0:T(128)} %constant.72) | copy-start | bytes 388
  7.6 14.7 %copy-start.12 = (f32[1,2]{1,0:T(1,128)S(1)}, f32[1,2]{1,0:T(1,128)}, u32[]{:S(2)}) copy-start(f32[1,2]{1,0:T(1,128)} %param.18) | copy-start | bytes 28
  7.6 15.3 %copy-start.5 = (f32[16,1,2,1024]{3,2,1,0:T(2,128)S(1)}, f32[16,1,2,1024]{3,2,1,0:T(2,128)}, u32[]{:S(2)}) copy-start(f32[16,1,2,1024]{3,2,1,0:T(2,128)} %param.13) | copy-start | bytes 393220
  8.6 137.1 %all-to-all-start = ((f32[2,2,1,2,49,256]{5,1,4,3,2,0:T(2,128)}), f32[2,2,1,2,49,256]{5,1,4,3,2,0:T(2,128)}, u32[]{:S(2)}, u32[]{:S(2)}) async-start(f32[2,2,1,2,49,256]{5,1,4,3,2,0:T(2,128)} %pad_maximum_fusion), calls=%async_computation | async-start | bytes 802816 | tf_op jit(solution)/shard_map/all_to_all | solution.py:100
  23.8 100.3 %copy-start.1 = (f32[16,1,2,32,32]{4,3,0,2,1:T(8,128)S(1)}, f32[16,1,2,32,32]{4,3,0,2,1:T(8,128)}, u32[]{:S(2)}) copy-start(f32[16,1,2,32,32]{4,3,0,2,1:T(8,128)} %reshape.284) | copy-start | bytes 393220
  50.6 1.2 copy-start.2
  50.6 1.4 copy-start.3
  87.4 1.2 copy-start.2
  87.4 1.4 copy-start.3
  130.5 4.1 %copy-start.6 = (f32[16,1,2,1024]{3,2,1,0:T(2,128)S(1)}, f32[16,1,2,1024]{3,2,1,0:T(2,128)}, u32[]{:S(2)}) copy-start(f32[16,1,2,1024]{3,2,1,0:T(2,128)} %param.13) | copy-start | bytes 393220
  131.9 15.0 %copy-start.10 = (f32[16,2]{0,1:T(2,128)S(1)}, f32[16,2]{0,1:T(2,128)}, u32[]{:S(2)}) copy-start(f32[16,2]{0,1:T(2,128)} %get-tuple-element.87) | copy-start | bytes 388
  133.6 15.1 %copy-start.11 = (f32[256]{0:T(256)S(1)}, f32[256]{0:T(256)}, u32[]{:S(2)}) copy-start(f32[256]{0:T(256)} %dynamic_slice.14) | copy-start | bytes 3076
  133.6 20.2 %copy-start.13 = (f32[16]{0:T(128)S(1)}, f32[16]{0:T(128)}, u32[]{:S(2)}) copy-start(f32[16]{0:T(128)} %get-tuple-element.86) | copy-start | bytes 196
  133.6 49.7 %copy-start.9 = (f32[16,256]{1,0:T(8,128)S(1)}, f32[16,256]{1,0:T(8,128)}, u32[]{:S(2)}) copy-start(f32[16,256]{1,0:T(8,128)} %param.22) | copy-start | bytes 49156
  133.6 49.8 %copy-start.15 = (pred[49]{0:T(512)(128)(4,1)S(1)}, pred[49]{0:T(512)(128)(4,1)}, u32[]{:S(2)}) copy-start(pred[49]{0:T(512)(128)(4,1)} %iota_compare_fusion) | copy-start | bytes 151
  133.6 49.9 %copy-start.8 = (f32[16,49,256]{2,0,1:T(8,128)S(1)}, f32[16,49,256]{2,0,1:T(8,128)}, u32[]{:S(2)}) copy-start(f32[16,49,256]{2,0,1:T(8,128)} %param.23) | copy-start | bytes 2408452
  148.7 35.9 %copy-start.4 = (f32[16,49,256]{2,0,1:T(8,128)}, f32[16,49,256]{2,0,1:T(8,128)S(1)}, u32[]{:S(2)}) copy-start(f32[16,49,256]{2,0,1:T(8,128)S(1)} %fusion.19) | copy-start | bytes 2408452
